TPU v7x, 256 devices: a whole 4x4x8 slice. The times are simulated.
256 devices in a mesh: band: 16 (over x_hi, y, core), spec: 16 (over z, x_lo).
Axes of the slice: x: 4 (x_hi: 2, x_lo: 2; x = x_hi * 2 + x_lo), y: 4, z: 8, core: 2. Of those that a mesh axis runs over, the one named last changes fastest.
Arguments:
- spectra: float32 [1296, 32, 2048], P(None, 'band', 'spec'), may hold values from 0.05 to 2
- sea_mask: int32 [32, 2048], P('band', 'spec'), may hold values 0 or 1
- wind: float32 [2, 32, 2048], P(None, None, ('spec', 'band')), may hold values from -30 to 30
- current: float32 [2, 32, 2048], P(None, None, ('spec', 'band')), may hold values from -0.2 to 0.2
Outputs:
- spectra_next: float32 [1296, 32, 2048], P(None, 'band', 'spec')
All inputs are finite; a program needn't handle non-finite values. No bound on the sum of `sea_mask` on one device may be relied on, other than what follows from the above.
Results may differ from a plain program's by a relative error of at most 0.0003.
Values sent between devices are 32-bit elements; how exact they have to be, the bound alone decides.
A program may use at most 128 MiB of HBM per device.

v0:
```python
import math

import jax
import jax.numpy as jnp
from jax import lax
from jax.sharding import PartitionSpec as P

NF = 36
ND = 36


LAT_SOUTH = 30.0
LAT_NORTH = 55.0
SPEED_TOP = 0.35
FREQ_STEP = 1.1
TURNING = 1.5
GROWTH = 0.05
WIND_COUPLING = 0.04


def padded(block, sides, width, periodic):
    for axis, dim in sides:
        count = lax.axis_size(axis)
        forward = [(i, i + 1) for i in range(count - 1)]
        if periodic:
            forward.append((count - 1, 0))
        backward = [(target, source) for source, target in forward]
        low = lax.ppermute(
            lax.slice_in_dim(block, block.shape[dim] - width, None, axis=dim), axis, forward
        )
        high = lax.ppermute(lax.slice_in_dim(block, 0, width, axis=dim), axis, backward)
        block = jnp.concatenate([low, block, high], axis=dim)
    return block


def latitude(position, total_rows):
    return (LAT_SOUTH + (LAT_NORTH - LAT_SOUTH) * position / total_rows) * (math.pi / 180.0)


def face_flux(behind, center, ahead, beyond, courant):
    forward = courant >= 0.0
    upwind = jnp.where(forward, behind, beyond)
    source_cell = jnp.where(forward, center, ahead)
    target_cell = jnp.where(forward, ahead, center)
    magnitude = jnp.abs(courant)
    face_value = (
        0.5 * (source_cell + target_cell)
        - 0.5 * magnitude * (target_cell - source_cell)
        - (1.0 - courant * courant) / 6.0 * (target_cell - 2.0 * source_cell + upwind)
    )
    return courant * face_value


def axis_fluxes(extended, cell_courant, along_axis):
    cell_count = extended.shape[along_axis] - 4

    def take_slice(values, offset):
        return lax.slice_in_dim(values, offset, offset + cell_count + 1, axis=along_axis)

    face_courant = 0.5 * (take_slice(cell_courant, 1) + take_slice(cell_courant, 2))
    return face_flux(
        take_slice(extended, 0),
        take_slice(extended, 1),
        take_slice(extended, 2),
        take_slice(extended, 3),
        face_courant,
    )


def component_tables(comp_index):
    freq_index = (comp_index // ND).astype(jnp.float32)
    direction = (comp_index % ND).astype(jnp.float32) * (2.0 * math.pi / ND)
    group_speed = SPEED_TOP * jnp.power(jnp.float32(FREQ_STEP), -freq_index)
    return (group_speed, jnp.cos(direction), jnp.sin(direction))


def propagate(spec_wide, spec_tall, current_wide, current_tall, comp_index, row_start, total_rows):
    group_speed, cos_dir, sin_dir = component_tables(comp_index)
    row_count = spec_wide.shape[1]
    cell_rows = (row_start + jnp.arange(row_count, dtype=jnp.int32)).astype(jnp.float32) + 0.5
    face_rows = (row_start + jnp.arange(row_count + 1, dtype=jnp.int32)).astype(jnp.float32)
    cell_cos = jnp.cos(latitude(cell_rows, total_rows))
    face_cos = jnp.cos(latitude(face_rows, total_rows))
    east_speed = (group_speed * cos_dir)[:, None, None] / cell_cos[None, :, None] + current_wide[0][
        None
    ]
    north_speed = (group_speed * sin_dir)[:, None, None] + current_tall[1][None]
    east_flux = axis_fluxes(spec_wide, east_speed, 2)
    north_flux = axis_fluxes(spec_tall, north_speed, 1) * face_cos[None, :, None]
    center_cells = spec_tall[:, 2:-2, :]
    return (
        center_cells
        - (east_flux[:, :, 1:] - east_flux[:, :, :-1])
        - (north_flux[:, 1:, :] - north_flux[:, :-1, :]) / cell_cos[None, :, None]
    )


def point_step(propagated, wind_rows, sea_rows, row_start, total_rows):
    row_count = propagated.shape[2]
    freq_index = jnp.arange(NF, dtype=jnp.int32).astype(jnp.float32)
    direction = jnp.arange(ND, dtype=jnp.int32).astype(jnp.float32) * (2.0 * math.pi / ND)
    group_speed = SPEED_TOP * jnp.power(jnp.float32(FREQ_STEP), -freq_index)
    cell_rows = (row_start + jnp.arange(row_count, dtype=jnp.int32)).astype(jnp.float32) + 0.5
    tangent = jnp.tan(latitude(cell_rows, total_rows))
    turn_rate = (
        -TURNING
        * group_speed[:, None, None]
        * jnp.cos(direction)[None, :, None]
        * tangent[None, None, :]
    )
    turn_wide = jnp.concatenate([turn_rate[:, -2:], turn_rate, turn_rate[:, :2]], axis=1)[..., None]
    spec_wide = jnp.concatenate([propagated[:, -2:], propagated, propagated[:, :2]], axis=1)
    turn_flux = axis_fluxes(spec_wide, turn_wide, 1)
    turned = propagated - (turn_flux[:, 1:] - turn_flux[:, :-1])
    wind_along = (
        wind_rows[0][None] * jnp.cos(direction)[:, None, None]
        + wind_rows[1][None] * jnp.sin(direction)[:, None, None]
    )
    coupling = WIND_COUPLING * jnp.power(jnp.float32(FREQ_STEP), freq_index)
    growth = GROWTH * jnp.maximum(wind_along[None] * coupling[:, None, None, None] - 1.0, 0.0)
    freq_weight = (freq_index + 1.0) / NF
    steepness = jnp.sum(freq_weight[:, None, None, None] * turned * turned, axis=(0, 1)) * (
        2.0 / (NF * ND)
    )
    damping = 1.0 + freq_weight[:, None, None, None] * steepness[None, None]
    return sea_rows[None, None] * turned * (1.0 + growth) / damping


def per_device(spectra, sea_mask, wind, current):
    comp_count, row_count, col_count = spectra.shape
    total_rows = row_count * lax.axis_size("band")
    band_index = lax.axis_index("band")
    row_start = band_index * row_count
    forcing = jnp.concatenate([wind, current], axis=0)
    relaid = lax.all_to_all(forcing, "band", split_axis=1, concat_axis=2, tiled=True)
    wind_here = relaid[:2]
    current_here = relaid[2:]
    sea_float = sea_mask.astype(jnp.float32)
    masked = spectra * sea_float[None]
    stacked = jnp.concatenate([masked, current_here], axis=0)
    cells_wide = padded(stacked, (("spec", 2),), 2, True)
    cells_tall = padded(stacked, (("band", 1),), 2, False)
    comp_index = jnp.arange(comp_count, dtype=jnp.int32)
    propagated = propagate(
        cells_wide[:comp_count],
        cells_tall[:comp_count],
        cells_wide[comp_count:],
        cells_tall[comp_count:],
        comp_index,
        row_start,
        total_rows,
    )
    shaped = propagated.reshape(NF, ND, row_count, col_count)
    result = point_step(shaped, wind_here, sea_float, row_start, total_rows)
    return result.reshape(comp_count, row_count, col_count)


def solution(mesh):
    placed = (
        P(None, "band", "spec"),
        P("band", "spec"),
        P(None, None, ("spec", "band")),
        P(None, None, ("spec", "band")),
    )
    return jax.shard_map(
        per_device, mesh=mesh, in_specs=placed, out_specs=P(None, "band", "spec"), check_vma=False
    )
```

profile of v0, /device:TPU:6, one launch (start us, length us, event | category | flops | bytes accessed | tf_op | source)
XLA Modules:
  0.0 103.3 jit_solution(9644188028851390996)
XLA Ops:
  0.0 0.7 pad_maximum_fusion.5
  0.7 0.7 copy.39
  1.4 7.5 %all-to-all-start = ((f32[4,32,8]{2,0,1:T(4,128)}), f32[4,32,8]{2,0,1:T(4,128)S(1)}, u32[]{:S(2)}, u32[]{:S(2)}) async-start(f32[4,32,8]{2,0,1:T(4,128)} %copy.39), calls=%async_computation | async-start | bytes 131072 | tf_op jit(solution)/shard_map/all_to_all | solution.py:135
  8.9 0.5 add_multiply_fusion
  10.4 0.7 convert_element_type.80
  11.1 1.4 %broadcast_multiply_fusion = f32[324,8,128]{2,1,0:T(8,128)S(1)} fusion(f32[324,8,128]{2,1,0:T(8,128)} %bitcast.36, f32[8,128]{1,0:T(8,128)S(1)} %bitcast.40), kind=kLoop, calls=%fused_computation.49 | loop fusion | flops 331776 | bytes 2658304 | tf_op jit(solution)/shard_map/mul | solution.py:139
  12.5 1.1 %broadcast_divide_fusion = f32[1296,2]{1,0:T(8,128)} fusion(f32[2]{0:T(128)S(1)} %fusion.46, f32[1296]{0:T(1024)S(1)} %fusion.38), kind=kLoop, calls=%fused_computation.50 | loop fusion | flops 2592 | bytes 15560 | tf_op jit(solution)/shard_map/div | solution.py:84
  13.6 1.1 %copy.49 = pred[36,37,2]{2,1,0:T(8,128)(4,1)} copy(pred[36,37,2]{1,2,0:T(4,128)(4,1)S(1)} %compare_bitcast_fusion) | data formatting | bytes 5328 | tf_op jit(solution)/shard_map/jit(_where)/broadcast_in_dim | solution.py:43
  15.1 1.2 %copy.50 = f32[36,37,2]{2,1,0:T(8,128)} copy(f32[36,37,2]{1,2,0:T(2,128)S(1)} %get-tuple-element.7) | data formatting | bytes 21312 | tf_op jit(solution)/shard_map/mul | solution.py:48
  16.3 1.2 %copy.48 = f32[36,37,2]{2,1,0:T(8,128)} copy(f32[36,37,2]{1,2,0:T(2,128)S(1)} %bitcast.37) | data formatting | bytes 21312 | tf_op jit(solution)/shard_map/mul | solution.py:51
  17.7 3.0 %pad_maximum_fusion.2 = f32[1298,2,128]{2,1,0:T(2,128)} fusion(f32[2,2,128]{2,1,0:T(2,128)S(1)} %slice.144, f32[1296,2,128]{2,1,0:T(2,128)S(1)} %bitcast.27), kind=kLoop, calls=%fused_computation.23 | loop fusion | flops 332288 | bytes 2658304 | tf_op jit(solution)/shard_map/concatenate | solution.py:140
  20.6 2.0 %collective-permute-start.2 = (f32[1298,2,128]{2,1,0:T(2,128)}, f32[1298,2,128]{2,1,0:T(2,128)}, u32[]{:S(2)}, u32[]{:S(2)}) collective-permute-start(f32[1298,2,128]{2,1,0:T(2,128)} %pad_maximum_fusion.2), channel_id=1, source_target_pairs={{0,16},{16,32},{32,48},{48,64},{64,80},{80,96},{96,112},{112,128},... | collective-permute-start | bytes 3987464 | tf_op jit(solution)/shard_map/ppermute | solution.py:28
  22.7 7.2 %collective-permute-start.3 = (f32[1298,2,128]{2,1,0:T(2,128)}, f32[1298,2,128]{2,1,0:T(2,128)}, u32[]{:S(2)}, u32[]{:S(2)}) collective-permute-start(f32[1298,2,128]{2,1,0:T(2,128)} %pad_maximum_fusion.2), channel_id=1, source_target_pairs={{16,0},{32,16},{48,32},{64,48},{80,64},{96,80},{112,96},{128,112},... | collective-permute-start | bytes 3987464 | tf_op jit(solution)/shard_map/ppermute | solution.py:31
  29.8 3.8 %fusion.18 = (f32[1298,2,2]{2,1,0:T(2,128)}, f32[1298,2,2]{2,1,0:T(2,128)S(1)}) fusion(f32[2,2,128]{2,1,0:T(2,128)S(1)} %slice.144, f32[1296,2,128]{2,1,0:T(2,128)S(1)} %bitcast.28), kind=kLoop, calls=%fused_computation.38 | loop fusion | flops 10384 | bytes 1370688 | tf_op jit(solution)/shard_map/concatenate | solution.py:140
  33.6 2.4 %copy.42 = f32[1298,2,2]{0,2,1:T(2,128)S(1)} copy(f32[1298,2,2]{2,1,0:T(2,128)} %get-tuple-element.11) | data formatting | bytes 41536 | tf_op jit(solution)/shard_map/slice | solution.py:29
  36.0 2.3 %collective-permute-start = (f32[1298,2,2]{0,2,1:T(2,128)S(1)}, f32[1298,2,2]{0,2,1:T(2,128)S(1)}, u32[]{:S(2)}, u32[]{:S(2)}) collective-permute-start(f32[1298,2,2]{0,2,1:T(2,128)S(1)} %copy.42), channel_id=1, source_target_pairs={{0,1},{1,2},{2,3},{3,4},{4,5},{5,6},{6,7},{7,8},{8,9},{9,10},{10,1... | collective-permute-start | bytes 62312 | tf_op jit(solution)/shard_map/ppermute | solution.py:28
  38.2 1.2 %copy.43 = f32[1298,2,2]{0,2,1:T(2,128)S(1)} copy(f32[1298,2,2]{2,1,0:T(2,128)S(1)} %get-tuple-element.12) | data formatting | bytes 41536 | tf_op jit(solution)/shard_map/slice | solution.py:31
  40.1 7.5 %collective-permute-done = f32[1298,2,2]{0,2,1:T(2,128)S(1)} collective-permute-done((f32[1298,2,2]{0,2,1:T(2,128)S(1)}, f32[1298,2,2]{0,2,1:T(2,128)S(1)}, u32[]{:S(2)}, u32[]{:S(2)}) %collective-permute-start) | collective-permute-done | bytes 20800 | tf_op jit(solution)/shard_map/ppermute | solution.py:28
  47.6 1.4 %copy.44 = f32[1298,2,2]{2,1,0:T(2,128)S(1)} copy(f32[1298,2,2]{0,2,1:T(2,128)S(1)} %collective-permute-done) | data formatting | bytes 41536 | tf_op jit(solution)/shard_map/ppermute | solution.py:28
  49.0 2.7 %copy.45 = f32[1298,2,2]{2,1,0:T(2,128)} copy(f32[1298,2,2]{0,2,1:T(2,128)} %collective-permute-done.1) | data formatting | bytes 41536 | tf_op jit(solution)/shard_map/ppermute | solution.py:31
  51.7 8.4 %maximum_maximum_fusion = (f32[1298,2,130]{2,1,0:T(2,128)S(1)}, f32[1298,2,130]{2,1,0:T(2,128)S(1)}) fusion(f32[2,2,128]{2,1,0:T(2,128)S(1)} %slice.144, f32[1296,2,128]{2,1,0:T(2,128)S(1)} %bitcast.29, f32[1298,2,2]{2,1,0:T(2,128)S(1)} %copy.44, f32[1298,2,2]{2,1,0:T(2,128)} %copy.45), kind=kLoop, calls=%fused_computation | loop fusion | flops 1349920 | bytes 4070528 | tf_op jit(solution)/shard_map/concatenate | solution.py:32
  60.2 1.0 copy-done.4
  61.2 1.6 %broadcast_add_fusion.1 = f32[1296,2,132]{2,1,0:T(2,128)S(1)} fusion(f32[2,132]{1,0:T(2,128)S(1)} %fusion.42, f32[1296,2]{1,0:T(8,128)S(1)} %copy-done.4), kind=kLoop, calls=%fused_computation.48 | loop fusion | flops 342144 | bytes 1380000 | tf_op jit(solution)/shard_map/add | solution.py:84
  62.8 11.6 %fusion.9 = f32[1296,2,129]{2,1,0:T(2,128)S(1)} fusion(f32[1298,2,130]{2,1,0:T(2,128)S(1)} %get-tuple-element.10, f32[1298,2,130]{2,1,0:T(2,128)S(1)} %get-tuple-element.9, f32[1296,2,132]{2,1,0:T(2,128)S(1)} %broadcast_add_fusion.1), kind=kLoop, calls=%fused_computation.16 | loop fusion | flops 7356096 | bytes 9362304 | tf_op jit(solution)/shard_map/mul | solution.py:51
  74.4 0.7 fusion.41
  75.1 3.5 %broadcast_add_fusion = f32[1296,6,128]{2,1,0:T(8,128)S(1)} fusion(f32[6,128]{1,0:T(8,128)S(1)} %fusion.41, f32[1296]{0:T(1024)S(1)} %fusion.39), kind=kLoop, calls=%fused_computation.19 | loop fusion | flops 995328 | bytes 3989568 | tf_op jit(solution)/shard_map/add | solution.py:87
  78.7 5.0 %maximum_maximum_fusion.1 = (f32[1298,4,128]{2,1,0:T(4,128)S(1)}, f32[1298,4,128]{2,1,0:T(4,128)S(1)}) fusion(f32[2,2,128]{2,1,0:T(2,128)S(1)} %slice.144, f32[1296,2,128]{2,1,0:T(2,128)S(1)} %bitcast.32, f32[1298,2,128]{2,1,0:T(2,128)} %collective-permute-done.2, f32[1298,2,128]{2,1,0:T(2,128)} %collective-permute-done.3), kind=kLoop, calls=%fused_computation.2 | loop fusion | flops 2658304 | bytes 9304064 | tf_op jit(solution)/shard_map/concatenate | solution.py:32
  83.7 5.4 %fusion.4 = f32[1296,3,128]{2,1,0:T(4,128)S(1)} fusion(f32[1298,4,128]{2,1,0:T(4,128)S(1)} %get-tuple-element.14, f32[1298,4,128]{2,1,0:T(4,128)S(1)} %get-tuple-element.13, f32[1296,6,128]{2,1,0:T(8,128)S(1)} %broadcast_add_fusion, f32[3]{0:T(128)S(1)} %multiply_cosine_fusion), kind=kLoop, calls=%fused_computation.9 | loop fusion | flops 11446272 | bytes 13934604 | tf_op jit(solution)/shard_map/mul | solution.py:89
  89.2 1.9 %divide_subtract_fusion = f32[1296,2,128]{2,1,0:T(2,128)S(1)} fusion(f32[1296,3,128]{2,1,0:T(4,128)S(1)} %fusion.4, f32[1296,2,129]{2,1,0:T(2,128)S(1)} %fusion.9, f32[2]{0:T(128)S(1)} %copy-done.10, f32[1296,2,128]{2,1,0:T(2,128)S(1)} %copy-done.1, f32[2,128]{1,0:T(2,128)S(1)} %copy-done.7), kind=kLoop, calls=%fused_computation.40 | loop fusion | flops 1990656 | bytes 7963656 | tf_op jit(solution)/shard_map/sub | solution.py:92
  91.1 7.3 %fusion.17 = f32[36,37,2,128]{3,2,1,0:T(2,128)S(1)} fusion(f32[36,2,2,128]{3,2,1,0:T(2,128)S(1)} %get-tuple-element.16, f32[36,36,2,128]{3,2,1,0:T(2,128)S(1)} %bitcast.34, f32[36,2,2,128]{3,2,1,0:T(2,128)S(1)} %get-tuple-element.15, pred[36,37,2]{2,1,0:T(8,128)(4,1)S(1)} %copy-done.5, f32[36,37,2]{2,1,0:T(8,128)S(1)} %copy.51, ...), kind=kLoop, calls=%fused_computation.37 | loop fusion | flops 6137856 | bytes 2873160 | tf_op jit(solution)/shard_map/mul | solution.py:51
  98.5 2.0 %fusion.20 = (f32[2,128]{1,0:T(2,128)S(1)}, f32[36,36,2,128]{3,2,1,0:T(2,128)S(1)}) fusion(f32[36]{0:T(128)S(1)} %copy-done.8, f32[36,36,2,128]{3,2,1,0:T(2,128)S(1)} %bitcast.35, f32[36,37,2,128]{3,2,1,0:T(2,128)S(1)} %fusion.17), kind=kLoop, calls=%fused_computation.41 | loop fusion | flops 1658624 | bytes 5309584 | tf_op jit(solution)/shard_map/reduce_sum | solution.py:122
  100.6 2.7 %multiply_divide_fusion = f32[36,36,2,128]{3,2,1,0:T(2,128)} fusion(f32[36,36,2,128]{3,2,1,0:T(2,128)S(1)} %get-tuple-element.6, f32[36,2,128]{2,1,0:T(2,128)S(1)} %multiply_add_fusion, f32[36,2,128]{2,1,0:T(2,128)S(1)} %multiply_add_fusion.1, f32[2,128]{1,0:T(2,128)S(1)} %copy-done.7, f32[36]{0:T(128)S(1)} %power_multiply_fusion), kind=kLoop, calls=%fused_computation.47 | loop fusion | flops 2654208 | bytes 2729104 | tf_op jit(solution)/shard_map/div | solution.py:126
  (57 shorter events, 2.3 us)
Async XLA Ops:
  1.4 16.1 %all-to-all-start = ((f32[4,32,8]{2,0,1:T(4,128)}), f32[4,32,8]{2,0,1:T(4,128)S(1)}, u32[]{:S(2)}, u32[]{:S(2)}) async-start(f32[4,32,8]{2,0,1:T(4,128)} %copy.39), calls=%async_computation | async-start | bytes 131072 | tf_op jit(solution)/shard_map/all_to_all | solution.py:135
  9.6 3.0 %copy-start.9 = (f32[2]{0:T(128)}, f32[2]{0:T(128)S(1)}, u32[]{:S(2)}) copy-start(f32[2]{0:T(128)S(1)} %fusion.46) | copy-start | bytes 28
  11.1 2.5 %copy-start.6 = (f32[2,128]{1,0:T(2,128)}, f32[2,128]{1,0:T(2,128)S(1)}, u32[]{:S(2)}) copy-start(f32[2,128]{1,0:T(2,128)S(1)} %convert_element_type.80) | copy-start | bytes 3076
  20.6 53.8 %collective-permute-start.2 = (f32[1298,2,128]{2,1,0:T(2,128)}, f32[1298,2,128]{2,1,0:T(2,128)}, u32[]{:S(2)}, u32[]{:S(2)}) collective-permute-start(f32[1298,2,128]{2,1,0:T(2,128)} %pad_maximum_fusion.2), channel_id=1, source_target_pairs={{0,16},{16,32},{32,48},{48,64},{64,80},{80,96},{96,112},{112,128},... | collective-permute-start | bytes 3987464 | tf_op jit(solution)/shard_map/ppermute | solution.py:28
  22.7 51.8 %collective-permute-start.3 = (f32[1298,2,128]{2,1,0:T(2,128)}, f32[1298,2,128]{2,1,0:T(2,128)}, u32[]{:S(2)}, u32[]{:S(2)}) collective-permute-start(f32[1298,2,128]{2,1,0:T(2,128)} %pad_maximum_fusion.2), channel_id=1, source_target_pairs={{16,0},{32,16},{48,32},{64,48},{80,64},{96,80},{112,96},{128,112},... | collective-permute-start | bytes 3987464 | tf_op jit(solution)/shard_map/ppermute | solution.py:31
  36.0 11.6 %collective-permute-start = (f32[1298,2,2]{0,2,1:T(2,128)S(1)}, f32[1298,2,2]{0,2,1:T(2,128)S(1)}, u32[]{:S(2)}, u32[]{:S(2)}) collective-permute-start(f32[1298,2,2]{0,2,1:T(2,128)S(1)} %copy.42), channel_id=1, source_target_pairs={{0,1},{1,2},{2,3},{3,4},{4,5},{5,6},{6,7},{7,8},{8,9},{9,10},{10,1... | collective-permute-start | bytes 62312 | tf_op jit(solution)/shard_map/ppermute | solution.py:28
  39.5 9.5 %collective-permute-start.1 = (f32[1298,2,2]{0,2,1:T(2,128)S(1)}, f32[1298,2,2]{0,2,1:T(2,128)}, u32[]{:S(2)}, u32[]{:S(2)}) collective-permute-start(f32[1298,2,2]{0,2,1:T(2,128)S(1)} %copy.43), channel_id=1, source_target_pairs={{1,0},{2,1},{3,2},{4,3},{5,4},{6,5},{7,6},{8,7},{9,8},{10,9},{11,1... | collective-permute-start | bytes 62312 | tf_op jit(solution)/shard_map/ppermute | solution.py:31
  51.7 8.4 %copy-start = (f32[1298,2,2]{2,1,0:T(2,128)S(1)}, f32[1298,2,2]{2,1,0:T(2,128)}, u32[]{:S(2)}) copy-start(f32[1298,2,2]{2,1,0:T(2,128)} %copy.45) | copy-start | bytes 62308
  60.1 1.1 %copy-start.4 = (f32[1296,2]{1,0:T(8,128)S(1)}, f32[1296,2]{1,0:T(8,128)}, u32[]{:S(2)}) copy-start(f32[1296,2]{1,0:T(8,128)} %broadcast_divide_fusion) | copy-start | bytes 31108
  83.7 5.4 %copy-start.1 = (f32[1296,2,128]{2,1,0:T(2,128)S(1)}, f32[1296,2,128]{2,1,0:T(2,128)}, u32[]{:S(2)}) copy-start(f32[1296,2,128]{2,1,0:T(2,128)} %param.4) | copy-start | bytes 3981316
  83.7 5.4 %copy-start.7 = (f32[2,128]{1,0:T(2,128)S(1)}, f32[2,128]{1,0:T(2,128)}, u32[]{:S(2)}) copy-start(f32[2,128]{1,0:T(2,128)} %copy-done.6) | copy-start | bytes 3076
  83.7 5.4 %copy-start.10 = (f32[2]{0:T(128)S(1)}, f32[2]{0:T(128)}, u32[]{:S(2)}) copy-start(f32[2]{0:T(128)} %copy-done.9) | copy-start | bytes 28
  89.1 2.0 %copy-start.2 = (f32[36,37,2]{2,1,0:T(8,128)S(1)}, f32[36,37,2]{2,1,0:T(8,128)}, u32[]{:S(2)}) copy-start(f32[36,37,2]{2,1,0:T(8,128)} %copy.50) | copy-start | bytes 31972
  89.1 2.0 %copy-start.3 = (f32[36,37,2]{2,1,0:T(8,128)S(1)}, f32[36,37,2]{2,1,0:T(8,128)}, u32[]{:S(2)}) copy-start(f32[36,37,2]{2,1,0:T(8,128)} %copy.48) | copy-start | bytes 31972
  89.1 2.0 %copy-start.5 = (pred[36,37,2]{2,1,0:T(8,128)(4,1)S(1)}, pred[36,37,2]{2,1,0:T(8,128)(4,1)}, u32[]{:S(2)}) copy-start(pred[36,37,2]{2,1,0:T(8,128)(4,1)} %copy.49) | copy-start | bytes 7996
  91.1 7.3 %copy-start.8 = (f32[36]{0:T(128)S(1)}, f32[36]{0:T(128)}, u32[]{:S(2)}) copy-start(f32[36]{0:T(128)} %add_multiply_fusion) | copy-start | bytes 436
where the time goes:
time: 104 us; the launch traced here: 103 us
  other arithmetic  62.5 us (60%)
  starting transfers between devices  19.1 us (18%)
  local copies, waits for them, and re-layouts  13.8 us (13%)
  waiting for transfers between devices  7.5 us (7%)
    mul x2, other arithmetic, face_flux(): return courant * face_value  18.9 us
    concatenate x2, other arithmetic, padded(): block = jnp.concatenate([low, block, high], axis=dim)  13.4 us
    ppermute x2, waiting for transfers between devices, padded(): lax.ppermute(lax.slice_in_dim(block, block.shape[dim] - width, None, axis...  7.49 us
    all_to_all x1, starting transfers between devices, per_device(): lax.all_to_all(forcing, 'band', split_axis=1, concat_axis=2, tiled=True)  7.45 us
    ppermute x2, starting transfers between devices, padded(): lax.ppermute(lax.slice_in_dim(block, 0, width, axis=dim), axis, backward)  7.42 us
    concatenate x2, other arithmetic, per_device(): stacked = jnp.concatenate([masked, current_here], axis=0)  6.74 us
    mul x1, other arithmetic, propagate(): axis_fluxes(spec_tall, north_speed, 1) * face_cos[None, :, None]  5.37 us
    ppermute x2, starting transfers between devices, padded(): lax.ppermute(lax.slice_in_dim(block, block.shape[dim] - width, None, axis...  4.27 us
  transfers between devices with their start and end apart: 5, of which 1 were waited for; matrix products, arithmetic and copies ran while one was open for 41% of the time, Pallas kernels for 0%

commit v1 on v0

v1 whole, which is shorter than its diff:
```python
import functools
import math

import jax
import jax.numpy as jnp
import numpy as np
from jax import lax
from jax.experimental import pallas as pl
from jax.experimental.pallas import tpu as pltpu
from jax.sharding import PartitionSpec as P

NF = 36
ND = 36

LAT_SOUTH = 30.0
LAT_NORTH = 55.0
SPEED_TOP = 0.35
FREQ_STEP = 1.1
TURNING = 1.5
GROWTH = 0.05
WIND_COUPLING = 0.04

MESH = pl.DeviceIdType.MESH
LANES = 128
ROWS = 2
VPF = ND * ROWS // 8
FPG = 3
GROUPS = NF // FPG
GROUP_ROWS = FPG * ND * ROWS
ROWS_ALL = NF * ND * ROWS


def tables(bands):
    total = bands * ROWS
    rad = math.pi / 180.0

    def lat(p):
        return (LAT_SOUTH + (LAT_NORTH - LAT_SOUTH) * p / total) * rad

    geo = np.zeros((bands, 8), np.float64)
    for b in range(bands):
        y = b * ROWS
        c0, c1 = math.cos(lat(y + 0.5)), math.cos(lat(y + 1.5))
        fs, fm, fn = math.cos(lat(y)), math.cos(lat(y + 1)), math.cos(lat(y + 2))
        geo[b] = [
            1.0 / c0, 1.0 / c1,
            0.5 * fs / c0, 0.5 * fm / c1,
            0.5 * fm / c0, 0.5 * fn / c1,
            math.tan(lat(y + 0.5)), math.tan(lat(y + 1.5)),
        ]
    f = np.arange(NF)
    speed = SPEED_TOP * FREQ_STEP ** (-f)
    wave = np.stack([speed, GROWTH * WIND_COUPLING * FREQ_STEP**f, (f + 1.0) / NF], 1)
    theta = 2.0 * math.pi * np.arange(ND) / ND
    cos, sin = np.cos(theta), np.sin(theta)
    turn = -TURNING * 0.5 * (np.roll(cos, 1) + cos)

    def spread(v):
        return np.broadcast_to(np.repeat(v, ROWS)[:, None], (ND * ROWS, LANES))

    trig = np.stack([spread(cos), spread(sin), spread(turn)]).astype(np.float32)
    return geo.astype(np.float32).reshape(-1), wave.astype(np.float32).reshape(-1), trig


def face(c, low, high, step, bend_low, bend_high):
    bend = jnp.where(c >= 0.0, bend_low, bend_high)
    return c * (((low + high) - c * step) + (c * c * (1.0 / 3.0) - 1.0 / 3.0) * bend)


def two_faces(c_low, c_high, low2, low, mid, high, high2):
    d0, d1, d2, d3 = low - low2, mid - low, high - mid, high2 - high
    k0, k1, k2 = d1 - d0, d2 - d1, d3 - d2
    return face(c_low, low, mid, d1, k0, k1), face(c_high, mid, high, d2, k1, k2)


def kernel(
    bands, specs,
    geo, wave, x_hbm, mask_ref, wind_ref, cur_ref, trig_ref,
    av, damp_ref,
    xv, south, north, mask_s, mask_n, square, strip, out_msg, in_msg, in_west, in_east,
    pack, pack_w, pack_e, cct, tnt, wnd, pbuf, fbuf,
    x_sem, msg_send, msg_recv, edge_send, edge_recv, pack_send, pack_recv, mask_send, mask_recv,
    n_send, s_send, n_recv, s_recv,
):
    b = lax.axis_index("band")
    s = lax.axis_index("spec")
    west, east = lax.rem(s + specs - 1, specs), lax.rem(s + 1, specs)
    has_n, has_s = b < bands - 1, b > 0
    up_band, down_band = jnp.minimum(b + 1, bands - 1), jnp.maximum(b - 1, 0)
    cols = LANES // bands

    barrier = pltpu.get_barrier_semaphore()
    for d in range(1, bands):
        pl.semaphore_signal(barrier, inc=1, device_id=(lax.rem(b + d, bands), s), device_id_type=MESH)
    for target in ((b, west), (b, east)):
        pl.semaphore_signal(barrier, inc=1, device_id=target, device_id_type=MESH)

    @pl.when(b < bands - 1)
    def _():
        pl.semaphore_signal(barrier, inc=1, device_id=(bands - 1, west), device_id_type=MESH)

    @pl.when(b > 0)
    def _():
        pl.semaphore_signal(barrier, inc=1, device_id=(0, east), device_id_type=MESH)

    load = pltpu.make_async_copy(x_hbm, xv, x_sem)
    load.start()

    sub = lax.broadcasted_iota(jnp.int32, (8, LANES), 0)
    lane = lax.broadcasted_iota(jnp.int32, (8, LANES), 1)
    even = lax.rem(sub, 2) == 0

    def pair(a, c):
        return jnp.where(even, a, c)

    square[...] = jnp.zeros_like(square)
    for i in range(2):
        square[i * 8 : i * 8 + cols, 0 : bands * ROWS] = wind_ref[i]
        square[16 + i * 8 : 16 + i * 8 + cols, 0 : bands * ROWS] = cur_ref[i]
    strip[...] = jnp.zeros_like(strip)
    strip[8 : 8 + bands * ROWS, :] = square[...].T[0 : bands * ROWS, :]
    message = strip[pl.ds(8, bands, stride=2), :]
    for q, first in ((1, 9), (2, 7), (3, 10)):
        message = message + pltpu.roll(strip[pl.ds(first, bands, stride=2), :], 32 * q, 1)
    for d in range(bands):
        out_msg[d] = message[d : d + 1]

    sea = mask_ref[...].astype(jnp.float32)
    sea_t = pair(sea[0:1], sea[1:2])

    load.wait()

    def pack_group(g, carry):
        acc = jnp.zeros((8, LANES), jnp.float32)
        for i in range(FPG * VPF):
            v = xv[pl.ds(pl.multiple_of(g * GROUP_ROWS + 8 * i, 8), 8), :] * sea_t
            acc = jnp.where((lane >= 4 * i) & (lane < 4 * i + 4), pltpu.roll(v, 4 * i + 2, 1), acc)
        pack[pl.ds(pl.multiple_of(g * 8, 8), 8), :] = acc
        return carry

    lax.fori_loop(0, GROUPS, pack_group, 0)

    at_end = (b == 0) | (b == bands - 1)

    @pl.when(at_end)
    def _():
        pl.semaphore_wait(barrier, 2 * bands)

    @pl.when(jnp.logical_not(at_end))
    def _():
        pl.semaphore_wait(barrier, bands + 1)

    def msg_copy(d, source):
        target = lax.rem(b + d, bands)
        return pltpu.make_async_remote_copy(
            src_ref=out_msg.at[target], dst_ref=in_msg.at[source], send_sem=msg_send.at[d], recv_sem=msg_recv.at[d],
            device_id=(target, s), device_id_type=MESH,
        )

    for d in range(1, bands):
        msg_copy(d, b).start()

    def edge_copy(t, to_east):
        return pltpu.make_async_remote_copy(
            src_ref=out_msg.at[t], dst_ref=in_west if to_east else in_east,
            send_sem=edge_send.at[t], recv_sem=edge_recv.at[0 if to_east else 1],
            device_id=(t, east if to_east else west), device_id_type=MESH,
        )

    @pl.when(b == bands - 1)
    def _():
        for t in range(bands):
            edge_copy(t, True).start()

    @pl.when(b == 0)
    def _():
        for t in range(bands):
            edge_copy(t, False).start()

    def chunk(g):
        return pl.ds(pl.multiple_of(g * GROUP_ROWS, GROUP_ROWS), GROUP_ROWS)

    def to_north(g):
        return pltpu.make_async_remote_copy(
            src_ref=x_hbm.at[chunk(g)], dst_ref=south.at[chunk(g)], send_sem=n_send.at[g], recv_sem=s_recv.at[g],
            device_id=(up_band, s), device_id_type=MESH,
        )

    def to_south(g):
        return pltpu.make_async_remote_copy(
            src_ref=x_hbm.at[chunk(g)], dst_ref=north.at[chunk(g)], send_sem=s_send.at[g], recv_sem=n_recv.at[g],
            device_id=(down_band, s), device_id_type=MESH,
        )

    def mask_copy(northward):
        return pltpu.make_async_remote_copy(
            src_ref=mask_ref, dst_ref=mask_s if northward else mask_n,
            send_sem=mask_send.at[0 if northward else 1], recv_sem=mask_recv.at[0 if northward else 1],
            device_id=(up_band if northward else down_band, s), device_id_type=MESH,
        )

    def pack_copy(to_east):
        return pltpu.make_async_remote_copy(
            src_ref=pack, dst_ref=pack_w if to_east else pack_e,
            send_sem=pack_send.at[0 if to_east else 1], recv_sem=pack_recv.at[0 if to_east else 1],
            device_id=(b, east if to_east else west), device_id_type=MESH,
        )

    @pl.when(has_n)
    def _():
        mask_copy(True).start()

    @pl.when(has_s)
    def _():
        mask_copy(False).start()

    pack_copy(True).start()
    pack_copy(False).start()

    def send_chunk(g, carry):
        @pl.when(has_n)
        def _():
            to_north(g).start()

        @pl.when(has_s)
        def _():
            to_south(g).start()

        return carry

    lax.fori_loop(0, GROUPS, send_chunk, 0)

    @pl.when(b == 0)
    def _():
        mask_s[...] = jnp.zeros_like(mask_s)

        def clear(i, carry):
            south[pl.ds(pl.multiple_of(i * GROUP_ROWS, 8), GROUP_ROWS), :] = jnp.zeros((GROUP_ROWS, LANES), jnp.float32)
            return carry

        lax.fori_loop(0, GROUPS, clear, 0)

    @pl.when(b == bands - 1)
    def _():
        mask_n[...] = jnp.zeros_like(mask_n)

        def clear(i, carry):
            north[pl.ds(pl.multiple_of(i * GROUP_ROWS, 8), GROUP_ROWS), :] = jnp.zeros((GROUP_ROWS, LANES), jnp.float32)
            return carry

        lax.fori_loop(0, GROUPS, clear, 0)

    g0 = b * 8
    inv_cos = pair(geo[g0], geo[g0 + 1])
    metric_a = pair(geo[g0 + 2], geo[g0 + 3])
    metric_b = pair(geo[g0 + 4], geo[g0 + 5])
    tangent = pair(geo[g0 + 6], geo[g0 + 7])
    for j in range(VPF):
        at = slice(8 * j, 8 * j + 8)
        cct[at, :] = trig_ref[0, at, :] * inv_cos
        tnt[at, :] = trig_ref[2, at, :] * tangent

    in_msg[b] = out_msg[b]
    for d in range(1, bands):
        msg_copy(d, lax.rem(b + bands - d, bands)).wait_recv()
    edge_copy(0, True).wait_recv()
    edge_copy(0, False).wait_recv()

    got = jnp.concatenate(
        [
            pltpu.roll(jnp.concatenate([in_msg[h + d] for d in range(8)], axis=0), h * cols, 1, stride=cols, stride_axis=0)
            for h in range(0, bands, 8)
        ],
        axis=0,
    )
    own = lax.broadcasted_iota(jnp.int32, (bands, LANES), 1) // cols == lax.broadcasted_iota(jnp.int32, (bands, LANES), 0)

    def field(q, f):
        moved = pltpu.roll(got, (LANES - 32 * q - 8 * f) % LANES, 1)
        return jnp.sum(jnp.where(own, moved, 0.0), axis=0, keepdims=True)

    w0 = pair(field(0, 0), field(1, 0))
    w1 = pair(field(0, 1), field(1, 1))
    u = pair(field(0, 2), field(1, 2))
    v0, v1, vs, vn = field(0, 3), field(1, 3), field(2, 3), field(3, 3)
    wm = jnp.broadcast_to(in_west[...], (8, LANES))
    em = jnp.broadcast_to(in_east[...], (8, LANES))
    u_w = pair(pltpu.roll(wm, LANES - 1 - (16 + cols - 1), 1), pltpu.roll(wm, LANES - 1 - (48 + cols - 1), 1))
    u_e = pair(pltpu.roll(em, LANES - 16, 1), pltpu.roll(em, LANES - 48, 1))
    c_west = 0.5 * (u + pltpu.roll(jnp.where(lane == LANES - 1, u_w, u), 1, 1))
    c_east = 0.5 * (u + pltpu.roll(jnp.where(lane == 0, u_e, u), LANES - 1, 1))
    c_south = 0.5 * pair(vs + v0, v0 + v1)
    c_north = 0.5 * pair(v0 + v1, v1 + vn)
    for j in range(VPF):
        at = slice(8 * j, 8 * j + 8)
        wnd[at, :] = w0 * trig_ref[0, at, :] + w1 * trig_ref[1, at, :]

    pack_copy(True).wait_recv()
    pack_copy(False).wait_recv()

    @pl.when(has_s)
    def _():
        mask_copy(True).wait_recv()

    @pl.when(has_n)
    def _():
        mask_copy(False).wait_recv()

    ms, mn = mask_s[...].astype(jnp.float32), mask_n[...].astype(jnp.float32)
    sea_s = pair(ms[0:1], ms[1:2])
    sea_n = pair(mn[0:1], mn[1:2])
    from_west = lax.rem(lane, 4) < 2

    def group(g, total):
        @pl.when(has_s)
        def _():
            to_north(g).wait_recv()

        @pl.when(has_n)
        def _():
            to_south(g).wait_recv()

        prow = pl.ds(pl.multiple_of(g * 8, 8), 8)
        beside = jnp.where(from_west, pack_w[prow, :], pack_e[prow, :])
        for k in range(FPG):
            f = g * FPG + k
            speed, growth, weight = wave[3 * f], wave[3 * f + 1], wave[3 * f + 2]
            base = g * GROUP_ROWS + k * ND * ROWS
            for j in range(VPF):
                at = slice(8 * j, 8 * j + 8)
                rows = pl.ds(pl.multiple_of(base + 8 * j, 8), 8)
                x = xv[rows, :] * sea_t
                halo = pltpu.roll(beside, LANES - (4 * (k * VPF + j) + 2), 1)
                w1, w2 = jnp.where(lane == LANES - 1, halo, x), jnp.where(lane >= LANES - 2, halo, x)
                e1, e2 = jnp.where(lane == 0, halo, x), jnp.where(lane < 2, halo, x)
                c = speed * cct[at, :]
                fw, fe = two_faces(
                    c + c_west, c + c_east,
                    pltpu.roll(w2, 2, 1), pltpu.roll(w1, 1, 1), x, pltpu.roll(e1, LANES - 1, 1), pltpu.roll(e2, LANES - 2, 1),
                )
                xs = south[rows, :] * sea_s
                xn = north[rows, :] * sea_n
                below = pair(pltpu.roll(xs, 7, 0), pltpu.roll(x, 1, 0))
                above = pair(pltpu.roll(x, 7, 0), pltpu.roll(xn, 1, 0))
                c = speed * trig_ref[1, at, :]
                fs, fn = two_faces(c + c_south, c + c_north, xs, below, x, above, xn)
                out = x - 0.5 * (fe - fw) - (metric_b * fn - metric_a * fs)
                pbuf[k, 8 + 8 * j : 16 + 8 * j, :] = out
                if j == 0:
                    pbuf[k, 8 + ND * ROWS : 16 + ND * ROWS, :] = out
                if j == VPF - 1:
                    pbuf[k, 0:8, :] = out
            for j in range(VPF):
                at = slice(8 * j, 8 * j + 8)
                o = 8 + 8 * j
                low2, low, mid, high = (pbuf[k, o + i : o + i + 8, :] for i in (-4, -2, 0, 2))
                d0, d1, d2 = low - low2, mid - low, high - mid
                flux = face(speed * tnt[at, :], low, mid, d1, d1 - d0, d2 - d1)
                fbuf[k, at, :] = flux
                if j == 0:
                    fbuf[k, ND * ROWS : ND * ROWS + 8, :] = flux
            square_sum = jnp.zeros((8, LANES), jnp.float32)
            for j in range(VPF):
                at = slice(8 * j, 8 * j + 8)
                rows = pl.ds(pl.multiple_of(base + 8 * j, 8), 8)
                turned = pbuf[k, 8 + 8 * j : 16 + 8 * j, :] - 0.5 * (fbuf[k, 8 * j + 2 : 8 * j + 10, :] - fbuf[k, at, :])
                square_sum = square_sum + turned * turned
                av[rows, :] = (sea_t * turned) * jnp.maximum(growth * wnd[at, :] + (1.0 - GROWTH), 1.0)
            total = total + weight * square_sum
        return total

    total = lax.fori_loop(0, GROUPS, group, jnp.zeros((8, LANES), jnp.float32))
    total = total + pltpu.roll(total, 4, 0)
    total = (total + pltpu.roll(total, 2, 0)) * (2.0 / (NF * ND))
    for f in range(NF):
        damp_ref[f] = 1.0 / (1.0 + total * ((f + 1.0) / NF))

    def finish(g, carry):
        @pl.when(has_n)
        def _():
            to_north(g).wait_send()

        @pl.when(has_s)
        def _():
            to_south(g).wait_send()

        return carry

    lax.fori_loop(0, GROUPS, finish, 0)
    for d in range(1, bands):
        msg_copy(d, b).wait_send()

    @pl.when(b == bands - 1)
    def _():
        for t in range(bands):
            edge_copy(t, True).wait_send()

    @pl.when(b == 0)
    def _():
        for t in range(bands):
            edge_copy(t, False).wait_send()

    pack_copy(True).wait_send()
    pack_copy(False).wait_send()

    @pl.when(has_n)
    def _():
        mask_copy(True).wait_send()

    @pl.when(has_s)
    def _():
        mask_copy(False).wait_send()


def damped(a_ref, damp_ref, o_hbm, ov, sem):
    for g in range(GROUPS):
        at = pl.ds(g * GROUP_ROWS, GROUP_ROWS)
        for k in range(FPG):
            factor = damp_ref[g * FPG + k]
            for j in range(VPF):
                rows = slice(g * GROUP_ROWS + 8 * (k * VPF + j), g * GROUP_ROWS + 8 * (k * VPF + j) + 8)
                ov[rows, :] = a_ref[rows, :] * factor
        pltpu.make_async_copy(ov.at[at], o_hbm.at[at], sem.at[g]).start()
    for g in range(GROUPS):
        at = pl.ds(g * GROUP_ROWS, GROUP_ROWS)
        pltpu.make_async_copy(ov.at[at], o_hbm.at[at], sem.at[g]).wait()


def per_device(bands, specs, spectra, sea_mask, wind, current):
    rows_all = ROWS_ALL
    geo, wave, trig = tables(bands)
    f32 = jnp.float32
    vmem = pl.BlockSpec(memory_space=pltpu.VMEM)
    smem = pl.BlockSpec(memory_space=pltpu.SMEM)
    hbm = pl.BlockSpec(memory_space=pl.ANY)
    dma = pltpu.SemaphoreType.DMA
    grown, damp = pl.pallas_call(
        functools.partial(kernel, bands, specs),
        out_shape=(
            pltpu.VMEM((rows_all, LANES), f32),
            pltpu.VMEM((NF, 8, LANES), f32),
        ),
        in_specs=[smem, smem, hbm, vmem, vmem, vmem, vmem],
        out_specs=(vmem, vmem),
        scratch_shapes=[
            pltpu.VMEM((rows_all, LANES), f32),
            pltpu.VMEM((rows_all, LANES), f32),
            pltpu.VMEM((rows_all, LANES), f32),
            pltpu.VMEM((ROWS, LANES), jnp.int32),
            pltpu.VMEM((ROWS, LANES), jnp.int32),
            pltpu.VMEM((LANES, LANES), f32),
            pltpu.VMEM((48, LANES), f32),
            pltpu.VMEM((bands, 1, LANES), f32),
            pltpu.VMEM((bands, 1, LANES), f32),
            pltpu.VMEM((1, LANES), f32),
            pltpu.VMEM((1, LANES), f32),
            pltpu.VMEM((GROUPS * 8, LANES), f32),
            pltpu.VMEM((GROUPS * 8, LANES), f32),
            pltpu.VMEM((GROUPS * 8, LANES), f32),
            pltpu.VMEM((ND * ROWS, LANES), f32),
            pltpu.VMEM((ND * ROWS, LANES), f32),
            pltpu.VMEM((ND * ROWS, LANES), f32),
            pltpu.VMEM((FPG, ND * ROWS + 16, LANES), f32),
            pltpu.VMEM((FPG, ND * ROWS + 8, LANES), f32),
            dma(()), dma((bands,)), dma((bands,)), dma((bands,)), dma((2,)),
            dma((2,)), dma((2,)), dma((2,)), dma((2,)),
            dma((GROUPS,)), dma((GROUPS,)), dma((GROUPS,)), dma((GROUPS,)),
        ],
        compiler_params=pltpu.CompilerParams(collective_id=0, has_side_effects=True),
        name="wave_step",
    )(
        jnp.asarray(geo), jnp.asarray(wave),
        spectra.reshape(rows_all, LANES), sea_mask,
        wind.transpose(0, 2, 1), current.transpose(0, 2, 1), jnp.asarray(trig),
    )
    out = pl.pallas_call(
        damped,
        out_shape=jax.ShapeDtypeStruct((rows_all, LANES), f32),
        in_specs=[vmem, vmem],
        out_specs=hbm,
        scratch_shapes=[pltpu.VMEM((rows_all, LANES), f32), dma((GROUPS,))],
        name="damped",
    )(*(pltpu.with_memory_space_constraint(v, pltpu.VMEM) for v in (grown, damp)))
    return out.reshape(NF * ND, ROWS, LANES)


def solution(mesh):
    placed = (
        P(None, "band", "spec"),
        P("band", "spec"),
        P(None, None, ("spec", "band")),
        P(None, None, ("spec", "band")),
    )
    return jax.shard_map(
        functools.partial(per_device, mesh.shape["band"], mesh.shape["spec"]),
        mesh=mesh, in_specs=placed, out_specs=P(None, "band", "spec"), check_vma=False,
    )
```

time: 104 us -> 29.6 us (0.28)
  the two profiles are of different devices: /device:TPU:6 before, /device:TPU:25 now
where the time goes in v1:
time: 29.6 us; the launch traced here: 29.5 us
  Pallas kernels  29.5 us (100%)
    pallas_call x1, Pallas kernels, per_device(): pl.pallas_call(functools.partial(kernel, bands, specs), out_shape=(pltpu....  28.3 us
    pallas_call x1, Pallas kernels, per_device(): pl.pallas_call(damped, out_shape=jax.ShapeDtypeStruct((rows_all, LANES),...  1.16 us

profile of v1, /device:TPU:25, one launch (start us, length us, event | category | flops | bytes accessed | tf_op | source)
XLA Modules:
  0.0 29.5 jit_solution(13263167290524253825)
XLA Ops:
  0.0 28.3 %wave_step.1 = (f32[2592,128]{1,0:T(8,128)S(1)}, f32[36,8,128]{2,1,0:T(8,128)S(1)}) custom-call(f32[128]{0:T(128)} %constant.6.clone.geo, f32[108]{0:T(128)} %constant.7.clone.wave, f32[2592,128]{1,0:T(8,128)} %bitcast.4, s32[2,128]{1,0:T(2,128)} %mask_ref.1, f32[2,8,32]{2,1,0:T(8,128)} %bitcast.5, f32[2,8,32]{2,1,0:T(8,128)} %bitcast.6, ...), custom_call_target="tpu_custom_call" | custom-call | tf_op jit(solution)/shard_map/wave_step/pallas_call | solution.py:437
  28.3 1.2 %damped.1 = f32[2592,128]{1,0:T(8,128)} custom-call(f32[2592,128]{1,0:T(8,128)S(1)} %get-tuple-element.7.a_ref, f32[36,8,128]{2,1,0:T(8,128)S(1)} %get-tuple-element.8.damp_ref), custom_call_target="tpu_custom_call" | custom-call | tf_op jit(solution)/shard_map/damped/pallas_call | solution.py:476

commit v2 on v1

--- a/solution.py
+++ b/solution.py
@@ -75,8 +75,9 @@
 
 def kernel(
     bands, specs,
-    geo, wave, x_hbm, mask_ref, wind_ref, cur_ref, trig_ref,
+    geo_hbm, wave_hbm, x_hbm, mask_hbm, wind_hbm, cur_hbm, trig_hbm,
     av, damp_ref,
+    geo, wave, mask_ref, wind_ref, cur_ref, trig_ref, small_sem,
     xv, south, north, mask_s, mask_n, square, strip, out_msg, in_msg, in_west, in_east,
     pack, pack_w, pack_e, cct, tnt, wnd, pbuf, fbuf,
     x_sem, msg_send, msg_recv, edge_send, edge_recv, pack_send, pack_recv, mask_send, mask_recv,
@@ -103,8 +104,19 @@
     def _():
         pl.semaphore_signal(barrier, inc=1, device_id=(0, east), device_id_type=MESH)
 
+    small = [
+        pltpu.make_async_copy(a, v, small_sem.at[i])
+        for i, (a, v) in enumerate((
+            (wind_hbm, wind_ref), (cur_hbm, cur_ref), (mask_hbm, mask_ref),
+            (geo_hbm, geo), (wave_hbm, wave), (trig_hbm, trig_ref),
+        ))
+    ]
+    for copy in small[:3]:
+        copy.start()
     load = pltpu.make_async_copy(x_hbm, xv, x_sem)
     load.start()
+    for copy in small[3:]:
+        copy.start()
 
     sub = lax.broadcasted_iota(jnp.int32, (8, LANES), 0)
     lane = lax.broadcasted_iota(jnp.int32, (8, LANES), 1)
@@ -114,6 +126,8 @@
         return jnp.where(even, a, c)
 
     square[...] = jnp.zeros_like(square)
+    for copy in small[:3]:
+        copy.wait()
     for i in range(2):
         square[i * 8 : i * 8 + cols, 0 : bands * ROWS] = wind_ref[i]
         square[16 + i * 8 : 16 + i * 8 + cols, 0 : bands * ROWS] = cur_ref[i]
@@ -250,6 +264,8 @@
 
         lax.fori_loop(0, GROUPS, clear, 0)
 
+    for copy in small[3:]:
+        copy.wait()
     g0 = b * 8
     inv_cos = pair(geo[g0], geo[g0 + 1])
     metric_a = pair(geo[g0 + 2], geo[g0 + 3])
@@ -431,7 +447,6 @@
     geo, wave, trig = tables(bands)
     f32 = jnp.float32
     vmem = pl.BlockSpec(memory_space=pltpu.VMEM)
-    smem = pl.BlockSpec(memory_space=pltpu.SMEM)
     hbm = pl.BlockSpec(memory_space=pl.ANY)
     dma = pltpu.SemaphoreType.DMA
     grown, damp = pl.pallas_call(
@@ -440,9 +455,16 @@
             pltpu.VMEM((rows_all, LANES), f32),
             pltpu.VMEM((NF, 8, LANES), f32),
         ),
-        in_specs=[smem, smem, hbm, vmem, vmem, vmem, vmem],
+        in_specs=[hbm] * 7,
         out_specs=(vmem, vmem),
         scratch_shapes=[
+            pltpu.SMEM(geo.shape, f32),
+            pltpu.SMEM(wave.shape, f32),
+            pltpu.VMEM((ROWS, LANES), jnp.int32),
+            pltpu.VMEM((2, LANES // bands, bands * ROWS), f32),
+            pltpu.VMEM((2, LANES // bands, bands * ROWS), f32),
+            pltpu.VMEM(trig.shape, f32),
+            dma((6,)),
             pltpu.VMEM((rows_all, LANES), f32),
             pltpu.VMEM((rows_all, LANES), f32),
             pltpu.VMEM((rows_all, LANES), f32),

time: 29.6 us -> 28.6 us (0.966)
  Pallas kernels: 29.5 us -> 28.5 us
    pallas_call x1, Pallas kernels: 28.3 us -> 27.3 us  [per_device(): pl.pallas_call(functools.partial(kernel, bands, specs), out_shape=(pltpu....]
where the time goes in v2:
time: 28.6 us; the launch traced here: 28.5 us
  Pallas kernels  28.5 us (100%)
    pallas_call x1, Pallas kernels, per_device(): pl.pallas_call(functools.partial(kernel, bands, specs), out_shape=(pltpu....  27.3 us
    pallas_call x1, Pallas kernels, per_device(): pl.pallas_call(damped, out_shape=jax.ShapeDtypeStruct((rows_all, LANES),...  1.16 us

profile of v2, /device:TPU:25, one launch (start us, length us, event | category | flops | bytes accessed | tf_op | source)
XLA Modules:
  0.0 28.5 jit_solution(10203410234063391285)
XLA Ops:
  0.0 27.3 %wave_step.1 = (f32[2592,128]{1,0:T(8,128)S(1)}, f32[36,8,128]{2,1,0:T(8,128)S(1)}) custom-call(f32[128]{0:T(128)} %constant.6.clone.geo_hbm, f32[108]{0:T(128)} %constant.7.clone.wave_hbm, f32[2592,128]{1,0:T(8,128)} %bitcast.4, s32[2,128]{1,0:T(2,128)} %mask_hbm.1, f32[2,8,32]{2,1,0:T(8,128)} %bitcast.5, f32[2,8,32]{2,1,0:T(8,128)} %bitcast.6, ...), custom_call_target="tpu_custom_call" | custom-call | tf_op jit(solution)/shard_map/wave_step/pallas_call | solution.py:452
  27.3 1.2 %damped.1 = f32[2592,128]{1,0:T(8,128)} custom-call(f32[2592,128]{1,0:T(8,128)S(1)} %get-tuple-element.7.a_ref, f32[36,8,128]{2,1,0:T(8,128)S(1)} %get-tuple-element.8.damp_ref), custom_call_target="tpu_custom_call" | custom-call | tf_op jit(solution)/shard_map/damped/pallas_call | solution.py:498

commit v3 on v2

--- a/solution.py
+++ b/solution.py
@@ -28,6 +28,7 @@
 GROUPS = NF // FPG
 GROUP_ROWS = FPG * ND * ROWS
 ROWS_ALL = NF * ND * ROWS
+FIRST_PART = 4
 
 
 def tables(bands):
@@ -78,9 +79,9 @@
     geo_hbm, wave_hbm, x_hbm, mask_hbm, wind_hbm, cur_hbm, trig_hbm,
     av, damp_ref,
     geo, wave, mask_ref, wind_ref, cur_ref, trig_ref, small_sem,
-    xv, south, north, mask_s, mask_n, square, strip, out_msg, in_msg, in_west, in_east,
+    xv, south, north, mask_s, mask_n, square, strip, out_raw, out_msg, in_msg, edge_in,
     pack, pack_w, pack_e, cct, tnt, wnd, pbuf, fbuf,
-    x_sem, msg_send, msg_recv, edge_send, edge_recv, pack_send, pack_recv, mask_send, mask_recv,
+    x_sem, msg_send, msg_recv, edge_sem, tokens, late, pack_send, pack_recv, mask_send, mask_recv,
     n_send, s_send, n_recv, s_recv,
 ):
     b = lax.axis_index("band")
@@ -91,18 +92,29 @@
     cols = LANES // bands
 
     barrier = pltpu.get_barrier_semaphore()
-    for d in range(1, bands):
-        pl.semaphore_signal(barrier, inc=1, device_id=(lax.rem(b + d, bands), s), device_id_type=MESH)
-    for target in ((b, west), (b, east)):
-        pl.semaphore_signal(barrier, inc=1, device_id=target, device_id_type=MESH)
-
-    @pl.when(b < bands - 1)
-    def _():
-        pl.semaphore_signal(barrier, inc=1, device_id=(bands - 1, west), device_id_type=MESH)
-
-    @pl.when(b > 0)
-    def _():
-        pl.semaphore_signal(barrier, inc=1, device_id=(0, east), device_id_type=MESH)
+    first_col, last_col = s == 0, s == specs - 1
+    pl.semaphore_signal(barrier, inc=1, device_id=(b, west), device_id_type=MESH)
+
+    @pl.when(jnp.logical_not(last_col))
+    def _():
+        pl.semaphore_signal(barrier, inc=1, device_id=(b, east), device_id_type=MESH)
+
+    def say(sem, target):
+        pl.semaphore_signal(sem, inc=1, device_id=(target, s), device_id_type=MESH)
+
+    partners = [b + bit - 2 * bit * lax.rem(b // bit, 2) for bit in (1, 2, 4, 8)]
+    for target in partners:
+        say(barrier, target)
+
+    odd = lax.rem(b, 2) == 1
+
+    @pl.when(odd & has_n)
+    def _():
+        say(barrier, up_band)
+
+    @pl.when(jnp.logical_not(odd) & has_s)
+    def _():
+        say(barrier, down_band)
 
     small = [
         pltpu.make_async_copy(a, v, small_sem.at[i])
@@ -137,6 +149,7 @@
     for q, first in ((1, 9), (2, 7), (3, 10)):
         message = message + pltpu.roll(strip[pl.ds(first, bands, stride=2), :], 32 * q, 1)
     for d in range(bands):
+        out_raw[d] = message[d : d + 1]
         out_msg[d] = message[d : d + 1]
 
     sea = mask_ref[...].astype(jnp.float32)
@@ -156,40 +169,29 @@
 
     at_end = (b == 0) | (b == bands - 1)
 
-    @pl.when(at_end)
-    def _():
-        pl.semaphore_wait(barrier, 2 * bands)
-
-    @pl.when(jnp.logical_not(at_end))
-    def _():
-        pl.semaphore_wait(barrier, bands + 1)
-
-    def msg_copy(d, source):
-        target = lax.rem(b + d, bands)
-        return pltpu.make_async_remote_copy(
-            src_ref=out_msg.at[target], dst_ref=in_msg.at[source], send_sem=msg_send.at[d], recv_sem=msg_recv.at[d],
-            device_id=(target, s), device_id_type=MESH,
-        )
-
-    for d in range(1, bands):
-        msg_copy(d, b).start()
-
-    def edge_copy(t, to_east):
-        return pltpu.make_async_remote_copy(
-            src_ref=out_msg.at[t], dst_ref=in_west if to_east else in_east,
-            send_sem=edge_send.at[t], recv_sem=edge_recv.at[0 if to_east else 1],
-            device_id=(t, east if to_east else west), device_id_type=MESH,
-        )
+    greeted = 7 - jnp.where(at_end, 1, 0) - jnp.where(first_col, 1, 0)
+    pl.semaphore_wait(barrier, greeted)
+
+    @pl.when(last_col)
+    def _():
+        pl.semaphore_signal(late.at[0], inc=1, device_id=(b, 0), device_id_type=MESH)
+
+    edge_to_east = pltpu.make_async_remote_copy(
+        src_ref=out_raw, dst_ref=edge_in, send_sem=edge_sem.at[0], recv_sem=edge_sem.at[1],
+        device_id=(b, east), device_id_type=MESH,
+    )
+    edge_to_west = pltpu.make_async_remote_copy(
+        src_ref=out_raw, dst_ref=edge_in, send_sem=edge_sem.at[0], recv_sem=edge_sem.at[1],
+        device_id=(b, west), device_id_type=MESH,
+    )
 
     @pl.when(b == bands - 1)
     def _():
-        for t in range(bands):
-            edge_copy(t, True).start()
-
-    @pl.when(b == 0)
-    def _():
-        for t in range(bands):
-            edge_copy(t, False).start()
+        edge_to_east.start()
+
+    @pl.when((b == 0) & jnp.logical_not(first_col))
+    def _():
+        edge_to_west.start()
 
     def chunk(g):
         return pl.ds(pl.multiple_of(g * GROUP_ROWS, GROUP_ROWS), GROUP_ROWS)
@@ -229,7 +231,10 @@
         mask_copy(False).start()
 
     pack_copy(True).start()
-    pack_copy(False).start()
+
+    @pl.when(jnp.logical_not(first_col))
+    def _():
+        pack_copy(False).start()
 
     def send_chunk(g, carry):
         @pl.when(has_n)
@@ -242,7 +247,46 @@
 
         return carry
 
-    lax.fori_loop(0, GROUPS, send_chunk, 0)
+    lax.fori_loop(0, FIRST_PART, send_chunk, 0)
+
+    for i in range(3):
+        say(tokens.at[i], partners[i])
+        pl.semaphore_wait(tokens.at[i], 1)
+
+    def msg_copy(target, source):
+        return pltpu.make_async_remote_copy(
+            src_ref=out_msg.at[target], dst_ref=in_msg.at[source],
+            send_sem=msg_send.at[target], recv_sem=msg_recv.at[source],
+            device_id=(target, s), device_id_type=MESH,
+        )
+
+    @pl.when(at_end)
+    def _():
+        edge_to_east.wait_recv()
+        edge = jnp.concatenate([edge_in[d] for d in range(bands)], axis=0)
+        wide = lax.broadcasted_iota(jnp.int32, (bands, LANES), 1)
+        last = (lax.broadcasted_iota(jnp.int32, (bands, LANES), 0) * 0 + b) > 0
+        first_row = jnp.where(last, pltpu.roll(edge, 64 - (16 + cols - 1), 1), pltpu.roll(edge, 64 - 16, 1))
+        second_row = jnp.where(last, pltpu.roll(edge, 65 - (48 + cols - 1), 1), pltpu.roll(edge, 65 - 48, 1))
+        plain = jnp.concatenate([out_raw[d] for d in range(bands)], axis=0)
+        merged = jnp.where(wide == 64, first_row, jnp.where(wide == 65, second_row, plain))
+        for d in range(bands):
+            out_msg[d] = merged[d : d + 1]
+
+    for d in range(1, bands):
+        msg_copy(lax.rem(b + d, bands), b).start()
+
+    @pl.when(first_col)
+    def _():
+        pl.semaphore_wait(late.at[0], 1)
+
+        @pl.when(b == 0)
+        def _():
+            edge_to_west.start()
+
+        pack_copy(False).start()
+
+    lax.fori_loop(FIRST_PART, GROUPS, send_chunk, 0)
 
     @pl.when(b == 0)
     def _():
@@ -278,9 +322,7 @@
 
     in_msg[b] = out_msg[b]
     for d in range(1, bands):
-        msg_copy(d, lax.rem(b + bands - d, bands)).wait_recv()
-    edge_copy(0, True).wait_recv()
-    edge_copy(0, False).wait_recv()
+        msg_copy(b, lax.rem(b + d, bands)).wait_recv()
 
     got = jnp.concatenate(
         [
@@ -299,10 +341,10 @@
     w1 = pair(field(0, 1), field(1, 1))
     u = pair(field(0, 2), field(1, 2))
     v0, v1, vs, vn = field(0, 3), field(1, 3), field(2, 3), field(3, 3)
-    wm = jnp.broadcast_to(in_west[...], (8, LANES))
-    em = jnp.broadcast_to(in_east[...], (8, LANES))
-    u_w = pair(pltpu.roll(wm, LANES - 1 - (16 + cols - 1), 1), pltpu.roll(wm, LANES - 1 - (48 + cols - 1), 1))
-    u_e = pair(pltpu.roll(em, LANES - 16, 1), pltpu.roll(em, LANES - 48, 1))
+    wm = jnp.broadcast_to(in_msg[bands - 1], (8, LANES))
+    em = jnp.broadcast_to(in_msg[0], (8, LANES))
+    u_w = pair(pltpu.roll(wm, LANES - 1 - 64, 1), pltpu.roll(wm, LANES - 1 - 65, 1))
+    u_e = pair(pltpu.roll(em, LANES - 64, 1), pltpu.roll(em, LANES - 65, 1))
     c_west = 0.5 * (u + pltpu.roll(jnp.where(lane == LANES - 1, u_w, u), 1, 1))
     c_east = 0.5 * (u + pltpu.roll(jnp.where(lane == 0, u_e, u), LANES - 1, 1))
     c_south = 0.5 * pair(vs + v0, v0 + v1)
@@ -404,17 +446,11 @@
 
     lax.fori_loop(0, GROUPS, finish, 0)
     for d in range(1, bands):
-        msg_copy(d, b).wait_send()
-
-    @pl.when(b == bands - 1)
-    def _():
-        for t in range(bands):
-            edge_copy(t, True).wait_send()
-
-    @pl.when(b == 0)
-    def _():
-        for t in range(bands):
-            edge_copy(t, False).wait_send()
+        msg_copy(lax.rem(b + d, bands), b).wait_send()
+
+    @pl.when(at_end)
+    def _():
+        edge_to_east.wait_send()
 
     pack_copy(True).wait_send()
     pack_copy(False).wait_send()
@@ -449,6 +485,7 @@
     vmem = pl.BlockSpec(memory_space=pltpu.VMEM)
     hbm = pl.BlockSpec(memory_space=pl.ANY)
     dma = pltpu.SemaphoreType.DMA
+    token = pltpu.SemaphoreType.REGULAR
     grown, damp = pl.pallas_call(
         functools.partial(kernel, bands, specs),
         out_shape=(
@@ -474,8 +511,8 @@
             pltpu.VMEM((48, LANES), f32),
             pltpu.VMEM((bands, 1, LANES), f32),
             pltpu.VMEM((bands, 1, LANES), f32),
-            pltpu.VMEM((1, LANES), f32),
-            pltpu.VMEM((1, LANES), f32),
+            pltpu.VMEM((bands, 1, LANES), f32),
+            pltpu.VMEM((bands, 1, LANES), f32),
             pltpu.VMEM((GROUPS * 8, LANES), f32),
             pltpu.VMEM((GROUPS * 8, LANES), f32),
             pltpu.VMEM((GROUPS * 8, LANES), f32),
@@ -484,7 +521,7 @@
             pltpu.VMEM((ND * ROWS, LANES), f32),
             pltpu.VMEM((FPG, ND * ROWS + 16, LANES), f32),
             pltpu.VMEM((FPG, ND * ROWS + 8, LANES), f32),
-            dma(()), dma((bands,)), dma((bands,)), dma((bands,)), dma((2,)),
+            dma(()), dma((bands,)), dma((bands,)), dma((2,)), token((3,)), token((1,)),
             dma((2,)), dma((2,)), dma((2,)), dma((2,)),
             dma((GROUPS,)), dma((GROUPS,)), dma((GROUPS,)), dma((GROUPS,)),
         ],

time: 28.6 us -> 26.6 us (0.930)
  Pallas kernels: 28.5 us -> 26.4 us
    pallas_call x1, Pallas kernels: 27.3 us -> 25.3 us  [per_device(): pl.pallas_call(functools.partial(kernel, bands, specs), out_shape=(pltpu....]
where the time goes in v3:
time: 26.6 us; the launch traced here: 26.4 us
  Pallas kernels  26.4 us (99%)
    pallas_call x1, Pallas kernels, per_device(): pl.pallas_call(functools.partial(kernel, bands, specs), out_shape=(pltpu....  25.3 us
    pallas_call x1, Pallas kernels, per_device(): pl.pallas_call(damped, out_shape=jax.ShapeDtypeStruct((rows_all, LANES),...  1.16 us

profile of v3, /device:TPU:25, one launch (start us, length us, event | category | flops | bytes accessed | tf_op | source)
XLA Modules:
  0.0 26.4 jit_solution(17286252727324650059)
XLA Ops:
  0.0 25.3 %wave_step.1 = (f32[2592,128]{1,0:T(8,128)S(1)}, f32[36,8,128]{2,1,0:T(8,128)S(1)}) custom-call(f32[128]{0:T(128)} %constant.6.clone.geo_hbm, f32[108]{0:T(128)} %constant.7.clone.wave_hbm, f32[2592,128]{1,0:T(8,128)} %bitcast.4, s32[2,128]{1,0:T(2,128)} %mask_hbm.1, f32[2,8,32]{2,1,0:T(8,128)} %bitcast.5, f32[2,8,32]{2,1,0:T(8,128)} %bitcast.6, ...), custom_call_target="tpu_custom_call" | custom-call | tf_op jit(solution)/shard_map/wave_step/pallas_call | solution.py:489
  25.3 1.2 %damped.1 = f32[2592,128]{1,0:T(8,128)} custom-call(f32[2592,128]{1,0:T(8,128)S(1)} %get-tuple-element.7.a_ref, f32[36,8,128]{2,1,0:T(8,128)S(1)} %get-tuple-element.8.damp_ref), custom_call_target="tpu_custom_call" | custom-call | tf_op jit(solution)/shard_map/damped/pallas_call | solution.py:535

commit v4 on v3

--- a/solution.py
+++ b/solution.py
@@ -28,7 +28,8 @@
 GROUPS = NF // FPG
 GROUP_ROWS = FPG * ND * ROWS
 ROWS_ALL = NF * ND * ROWS
-FIRST_PART = 4
+PARTS = (5, 3, 2, 1, 1)
+FIRST_PART = 1
 
 
 def tables(bands):
@@ -79,9 +80,9 @@
     geo_hbm, wave_hbm, x_hbm, mask_hbm, wind_hbm, cur_hbm, trig_hbm,
     av, damp_ref,
     geo, wave, mask_ref, wind_ref, cur_ref, trig_ref, small_sem,
-    xv, south, north, mask_s, mask_n, square, strip, out_raw, out_msg, in_msg, edge_in,
-    pack, pack_w, pack_e, cct, tnt, wnd, pbuf, fbuf,
-    x_sem, msg_send, msg_recv, edge_sem, tokens, late, pack_send, pack_recv, mask_send, mask_recv,
+    xv, south, north, mask_s, mask_n, square, strip, out_raw, out_msg, in_msg, edge_in, far_edge,
+    pack, go_east, go_west, pack_w, pack_e, cct, tnt, wnd, pbuf, fbuf,
+    x_sem, msg_send, msg_recv, edge_sem, far_send, tokens, late, pack_send, pack_recv, mask_send, mask_recv,
     n_send, s_send, n_recv, s_recv,
 ):
     b = lax.axis_index("band")
@@ -103,8 +104,13 @@
         pl.semaphore_signal(sem, inc=1, device_id=(target, s), device_id_type=MESH)
 
     partners = [b + bit - 2 * bit * lax.rem(b // bit, 2) for bit in (1, 2, 4, 8)]
-    for target in partners:
-        say(barrier, target)
+    has_bit = [lax.rem(b // bit, 2) == 1 for bit in (1, 2, 4, 8)]
+    say(barrier, partners[0])
+    for i in range(1, 4):
+
+        @pl.when(jnp.logical_not(has_bit[i]))
+        def _(i=i):
+            say(barrier, partners[i])
 
     odd = lax.rem(b, 2) == 1
 
@@ -115,6 +121,10 @@
     @pl.when(jnp.logical_not(odd) & has_s)
     def _():
         say(barrier, down_band)
+
+    @pl.when(first_col & (b < bands - 1))
+    def _():
+        pl.semaphore_signal(barrier, inc=1, device_id=(bands - 1, west), device_id_type=MESH)
 
     small = [
         pltpu.make_async_copy(a, v, small_sem.at[i])
@@ -167,10 +177,25 @@
 
     lax.fori_loop(0, GROUPS, pack_group, 0)
 
+    low_half = lax.rem(lane, 4) < 2
+    for i in range(GROUPS // 2):
+        two = [pack[16 * i + 8 * r : 16 * i + 8 * r + 8, :] for r in range(2)]
+        at = slice(8 * i, 8 * i + 8)
+        go_east[at, :] = jnp.where(low_half, two[0], pltpu.roll(two[1], 2, 1))
+        go_west[at, :] = jnp.where(low_half, pltpu.roll(two[0], LANES - 2, 1), two[1])
+
     at_end = (b == 0) | (b == bands - 1)
 
-    greeted = 7 - jnp.where(at_end, 1, 0) - jnp.where(first_col, 1, 0)
+    far_corner = last_col & (b == bands - 1)
+    greeted = 4 - jnp.where(at_end, 1, 0) - jnp.where(first_col, 1, 0) + jnp.where(far_corner, bands - 1, 0)
+    for i in range(1, 4):
+        greeted = greeted + jnp.where(has_bit[i], 1, 0)
     pl.semaphore_wait(barrier, greeted)
+    for i in range(1, 4):
+
+        @pl.when(has_bit[i])
+        def _(i=i):
+            say(late.at[i], partners[i])
 
     @pl.when(last_col)
     def _():
@@ -185,26 +210,45 @@
         device_id=(b, west), device_id_type=MESH,
     )
 
-    @pl.when(b == bands - 1)
+    def far_copy(t):
+        return pltpu.make_async_remote_copy(
+            src_ref=out_raw.at[t], dst_ref=far_edge, send_sem=far_send.at[t], recv_sem=edge_sem.at[2],
+            device_id=(t, 0), device_id_type=MESH,
+        )
+
+    @pl.when(far_corner)
+    def _():
+        for t in range(bands):
+            far_copy(t).start()
+
+    passes_east = (b == bands - 1) & jnp.logical_not(last_col)
+
+    @pl.when(passes_east)
     def _():
         edge_to_east.start()
 
+    @pl.when(jnp.logical_not(first_col))
+    def _():
+        far_edge[...] = jnp.zeros_like(far_edge)
+
     @pl.when((b == 0) & jnp.logical_not(first_col))
     def _():
         edge_to_west.start()
 
-    def chunk(g):
-        return pl.ds(pl.multiple_of(g * GROUP_ROWS, GROUP_ROWS), GROUP_ROWS)
-
-    def to_north(g):
+    firsts = [sum(PARTS[:i]) for i in range(len(PARTS))]
+
+    def part(i):
+        return pl.ds(firsts[i] * GROUP_ROWS, PARTS[i] * GROUP_ROWS)
+
+    def to_north(i):
         return pltpu.make_async_remote_copy(
-            src_ref=x_hbm.at[chunk(g)], dst_ref=south.at[chunk(g)], send_sem=n_send.at[g], recv_sem=s_recv.at[g],
+            src_ref=x_hbm.at[part(i)], dst_ref=south.at[part(i)], send_sem=n_send.at[i], recv_sem=s_recv.at[i],
             device_id=(up_band, s), device_id_type=MESH,
         )
 
-    def to_south(g):
+    def to_south(i):
         return pltpu.make_async_remote_copy(
-            src_ref=x_hbm.at[chunk(g)], dst_ref=north.at[chunk(g)], send_sem=s_send.at[g], recv_sem=n_recv.at[g],
+            src_ref=x_hbm.at[part(i)], dst_ref=north.at[part(i)], send_sem=s_send.at[i], recv_sem=n_recv.at[i],
             device_id=(down_band, s), device_id_type=MESH,
         )
 
@@ -217,7 +261,7 @@
 
     def pack_copy(to_east):
         return pltpu.make_async_remote_copy(
-            src_ref=pack, dst_ref=pack_w if to_east else pack_e,
+            src_ref=go_east if to_east else go_west, dst_ref=pack_w if to_east else pack_e,
             send_sem=pack_send.at[0 if to_east else 1], recv_sem=pack_recv.at[0 if to_east else 1],
             device_id=(b, east if to_east else west), device_id_type=MESH,
         )
@@ -236,18 +280,24 @@
     def _():
         pack_copy(False).start()
 
-    def send_chunk(g, carry):
-        @pl.when(has_n)
-        def _():
-            to_north(g).start()
-
-        @pl.when(has_s)
-        def _():
-            to_south(g).start()
-
-        return carry
-
-    lax.fori_loop(0, FIRST_PART, send_chunk, 0)
+    def send_parts(some):
+        for i in some:
+
+            @pl.when(has_n)
+            def _(i=i):
+                to_north(i).start()
+
+            @pl.when(has_s)
+            def _(i=i):
+                to_south(i).start()
+
+    send_parts(range(FIRST_PART))
+
+    for i in range(1, 4):
+
+        @pl.when(jnp.logical_not(has_bit[i]))
+        def _(i=i):
+            pl.semaphore_wait(late.at[i], 1)
 
     for i in range(3):
         say(tokens.at[i], partners[i])
@@ -260,7 +310,7 @@
             device_id=(target, s), device_id_type=MESH,
         )
 
-    @pl.when(at_end)
+    @pl.when((b == 0) | ((b == bands - 1) & jnp.logical_not(first_col)))
     def _():
         edge_to_east.wait_recv()
         edge = jnp.concatenate([edge_in[d] for d in range(bands)], axis=0)
@@ -286,7 +336,7 @@
 
         pack_copy(False).start()
 
-    lax.fori_loop(FIRST_PART, GROUPS, send_chunk, 0)
+    send_parts(range(FIRST_PART, len(PARTS)))
 
     @pl.when(b == 0)
     def _():
@@ -341,9 +391,18 @@
     w1 = pair(field(0, 1), field(1, 1))
     u = pair(field(0, 2), field(1, 2))
     v0, v1, vs, vn = field(0, 3), field(1, 3), field(2, 3), field(3, 3)
+    @pl.when(first_col)
+    def _():
+        far_copy(0).wait_recv()
+
     wm = jnp.broadcast_to(in_msg[bands - 1], (8, LANES))
+    fm = jnp.broadcast_to(far_edge[...], (8, LANES))
     em = jnp.broadcast_to(in_msg[0], (8, LANES))
-    u_w = pair(pltpu.roll(wm, LANES - 1 - 64, 1), pltpu.roll(wm, LANES - 1 - 65, 1))
+    u_w = jnp.where(
+        jnp.zeros_like(lane) + s == 0,
+        pair(pltpu.roll(fm, LANES - 1 - (16 + cols - 1), 1), pltpu.roll(fm, LANES - 1 - (48 + cols - 1), 1)),
+        pair(pltpu.roll(wm, LANES - 1 - 64, 1), pltpu.roll(wm, LANES - 1 - 65, 1)),
+    )
     u_e = pair(pltpu.roll(em, LANES - 64, 1), pltpu.roll(em, LANES - 65, 1))
     c_west = 0.5 * (u + pltpu.roll(jnp.where(lane == LANES - 1, u_w, u), 1, 1))
     c_east = 0.5 * (u + pltpu.roll(jnp.where(lane == 0, u_e, u), LANES - 1, 1))
@@ -367,19 +426,25 @@
     ms, mn = mask_s[...].astype(jnp.float32), mask_n[...].astype(jnp.float32)
     sea_s = pair(ms[0:1], ms[1:2])
     sea_n = pair(mn[0:1], mn[1:2])
-    from_west = lax.rem(lane, 4) < 2
+    for i in range(GROUPS // 2):
+        at = slice(8 * i, 8 * i + 8)
+        pw, pe = pack_w[at, :], pack_e[at, :]
+        pack[16 * i : 16 * i + 8, :] = jnp.where(low_half, pw, pltpu.roll(pe, 2, 1))
+        pack[16 * i + 8 : 16 * i + 16, :] = jnp.where(low_half, pltpu.roll(pw, LANES - 2, 1), pe)
 
     def group(g, total):
-        @pl.when(has_s)
-        def _():
-            to_north(g).wait_recv()
-
-        @pl.when(has_n)
-        def _():
-            to_south(g).wait_recv()
+        for i, first in enumerate(firsts):
+
+            @pl.when((g == first) & has_s)
+            def _(i=i):
+                to_north(i).wait_recv()
+
+            @pl.when((g == first) & has_n)
+            def _(i=i):
+                to_south(i).wait_recv()
 
         prow = pl.ds(pl.multiple_of(g * 8, 8), 8)
-        beside = jnp.where(from_west, pack_w[prow, :], pack_e[prow, :])
+        beside = pack[prow, :]
         for k in range(FPG):
             f = g * FPG + k
             speed, growth, weight = wave[3 * f], wave[3 * f + 1], wave[3 * f + 2]
@@ -433,24 +498,27 @@
     for f in range(NF):
         damp_ref[f] = 1.0 / (1.0 + total * ((f + 1.0) / NF))
 
-    def finish(g, carry):
+    for i in range(len(PARTS)):
+
         @pl.when(has_n)
-        def _():
-            to_north(g).wait_send()
+        def _(i=i):
+            to_north(i).wait_send()
 
         @pl.when(has_s)
-        def _():
-            to_south(g).wait_send()
-
-        return carry
-
-    lax.fori_loop(0, GROUPS, finish, 0)
+        def _(i=i):
+            to_south(i).wait_send()
+
     for d in range(1, bands):
         msg_copy(lax.rem(b + d, bands), b).wait_send()
 
-    @pl.when(at_end)
+    @pl.when((b == 0) | passes_east)
     def _():
         edge_to_east.wait_send()
+
+    @pl.when(far_corner)
+    def _():
+        for t in range(bands):
+            far_copy(t).wait_send()
 
     pack_copy(True).wait_send()
     pack_copy(False).wait_send()
@@ -513,17 +581,20 @@
             pltpu.VMEM((bands, 1, LANES), f32),
             pltpu.VMEM((bands, 1, LANES), f32),
             pltpu.VMEM((bands, 1, LANES), f32),
+            pltpu.VMEM((1, LANES), f32),
             pltpu.VMEM((GROUPS * 8, LANES), f32),
-            pltpu.VMEM((GROUPS * 8, LANES), f32),
-            pltpu.VMEM((GROUPS * 8, LANES), f32),
+            pltpu.VMEM((GROUPS * 4, LANES), f32),
+            pltpu.VMEM((GROUPS * 4, LANES), f32),
+            pltpu.VMEM((GROUPS * 4, LANES), f32),
+            pltpu.VMEM((GROUPS * 4, LANES), f32),
             pltpu.VMEM((ND * ROWS, LANES), f32),
             pltpu.VMEM((ND * ROWS, LANES), f32),
             pltpu.VMEM((ND * ROWS, LANES), f32),
             pltpu.VMEM((FPG, ND * ROWS + 16, LANES), f32),
             pltpu.VMEM((FPG, ND * ROWS + 8, LANES), f32),
-            dma(()), dma((bands,)), dma((bands,)), dma((2,)), token((3,)), token((1,)),
+            dma(()), dma((bands,)), dma((bands,)), dma((3,)), dma((bands,)), token((3,)), token((4,)),
             dma((2,)), dma((2,)), dma((2,)), dma((2,)),
-            dma((GROUPS,)), dma((GROUPS,)), dma((GROUPS,)), dma((GROUPS,)),
+            *(dma((len(PARTS),)) for _ in range(4)),
         ],
         compiler_params=pltpu.CompilerParams(collective_id=0, has_side_effects=True),
         name="wave_step",

time: 26.6 us -> 25.4 us (0.955)
  Pallas kernels: 26.4 us -> 25.1 us
    pallas_call x1, Pallas kernels: 25.3 us -> 24 us  [per_device(): pl.pallas_call(functools.partial(kernel, bands, specs), out_shape=(pltpu....]
where the time goes in v4:
time: 25.4 us; the launch traced here: 25.1 us
  Pallas kernels  25.1 us (99%)
    pallas_call x1, Pallas kernels, per_device(): pl.pallas_call(functools.partial(kernel, bands, specs), out_shape=(pltpu....  24 us
    pallas_call x1, Pallas kernels, per_device(): pl.pallas_call(damped, out_shape=jax.ShapeDtypeStruct((rows_all, LANES),...  1.16 us

profile of v4, /device:TPU:25, one launch (start us, length us, event | category | flops | bytes accessed | tf_op | source)
XLA Modules:
  0.0 25.1 jit_solution(8677274265781938852)
XLA Ops:
  0.0 24.0 %wave_step.1 = (f32[2592,128]{1,0:T(8,128)S(1)}, f32[36,8,128]{2,1,0:T(8,128)S(1)}) custom-call(f32[128]{0:T(128)} %constant.6.clone.geo_hbm, f32[108]{0:T(128)} %constant.7.clone.wave_hbm, f32[2592,128]{1,0:T(8,128)} %bitcast.4, s32[2,128]{1,0:T(2,128)} %mask_hbm.1, f32[2,8,32]{2,1,0:T(8,128)} %bitcast.5, f32[2,8,32]{2,1,0:T(8,128)} %bitcast.6, ...), custom_call_target="tpu_custom_call" | custom-call | tf_op jit(solution)/shard_map/wave_step/pallas_call | solution.py:557
  24.0 1.2 %damped.1 = f32[2592,128]{1,0:T(8,128)} custom-call(f32[2592,128]{1,0:T(8,128)S(1)} %get-tuple-element.7.a_ref, f32[36,8,128]{2,1,0:T(8,128)S(1)} %get-tuple-element.8.damp_ref), custom_call_target="tpu_custom_call" | custom-call | tf_op jit(solution)/shard_map/damped/pallas_call | solution.py:606

commit v5 on v4

--- a/solution.py
+++ b/solution.py
@@ -28,7 +28,7 @@
 GROUPS = NF // FPG
 GROUP_ROWS = FPG * ND * ROWS
 ROWS_ALL = NF * ND * ROWS
-PARTS = (5, 3, 2, 1, 1)
+PARTS = (15, 9, 6, 3, 2, 1)
 FIRST_PART = 1
 
 
@@ -238,7 +238,7 @@
     firsts = [sum(PARTS[:i]) for i in range(len(PARTS))]
 
     def part(i):
-        return pl.ds(firsts[i] * GROUP_ROWS, PARTS[i] * GROUP_ROWS)
+        return pl.ds(firsts[i] * ND * ROWS, PARTS[i] * ND * ROWS)
 
     def to_north(i):
         return pltpu.make_async_remote_copy(
@@ -432,21 +432,25 @@
         pack[16 * i : 16 * i + 8, :] = jnp.where(low_half, pw, pltpu.roll(pe, 2, 1))
         pack[16 * i + 8 : 16 * i + 16, :] = jnp.where(low_half, pltpu.roll(pw, LANES - 2, 1), pe)
 
-    def group(g, total):
+    def arrived(f):
         for i, first in enumerate(firsts):
 
-            @pl.when((g == first) & has_s)
+            @pl.when((f == first) & has_s)
             def _(i=i):
                 to_north(i).wait_recv()
 
-            @pl.when((g == first) & has_n)
+            @pl.when((f == first) & has_n)
             def _(i=i):
                 to_south(i).wait_recv()
 
+    def group(g, total, last=False):
+        arrived(g * FPG)
         prow = pl.ds(pl.multiple_of(g * 8, 8), 8)
         beside = pack[prow, :]
         for k in range(FPG):
             f = g * FPG + k
+            if last and k:
+                arrived(f)
             speed, growth, weight = wave[3 * f], wave[3 * f + 1], wave[3 * f + 2]
             base = g * GROUP_ROWS + k * ND * ROWS
             for j in range(VPF):
@@ -492,7 +496,8 @@
             total = total + weight * square_sum
         return total
 
-    total = lax.fori_loop(0, GROUPS, group, jnp.zeros((8, LANES), jnp.float32))
+    total = lax.fori_loop(0, GROUPS - 1, group, jnp.zeros((8, LANES), jnp.float32))
+    total = group(jnp.int32(GROUPS - 1), total, last=True)
     total = total + pltpu.roll(total, 4, 0)
     total = (total + pltpu.roll(total, 2, 0)) * (2.0 / (NF * ND))
     for f in range(NF):

time: 25.4 us -> 25.1 us (0.988)
  Pallas kernels: 25.1 us -> 24.8 us
    pallas_call x1, Pallas kernels: 24 us -> 23.7 us  [per_device(): pl.pallas_call(functools.partial(kernel, bands, specs), out_shape=(pltpu....]
where the time goes in v5:
time: 25.1 us; the launch traced here: 24.9 us
  Pallas kernels  24.8 us (99%)
    pallas_call x1, Pallas kernels, per_device(): pl.pallas_call(functools.partial(kernel, bands, specs), out_shape=(pltpu....  23.7 us
    pallas_call x1, Pallas kernels, per_device(): pl.pallas_call(damped, out_shape=jax.ShapeDtypeStruct((rows_all, LANES),...  1.16 us

profile of v5, /device:TPU:25, one launch (start us, length us, event | category | flops | bytes accessed | tf_op | source)
XLA Modules:
  0.0 24.9 jit_solution(1094242199707686351)
XLA Ops:
  0.0 23.7 %wave_step.1 = (f32[2592,128]{1,0:T(8,128)S(1)}, f32[36,8,128]{2,1,0:T(8,128)S(1)}) custom-call(f32[128]{0:T(128)} %constant.6.clone.geo_hbm, f32[108]{0:T(128)} %constant.7.clone.wave_hbm, f32[2592,128]{1,0:T(8,128)} %bitcast.4, s32[2,128]{1,0:T(2,128)} %mask_hbm.1, f32[2,8,32]{2,1,0:T(8,128)} %bitcast.5, f32[2,8,32]{2,1,0:T(8,128)} %bitcast.6, ...), custom_call_target="tpu_custom_call" | custom-call | tf_op jit(solution)/shard_map/wave_step/pallas_call | solution.py:562
  23.7 1.2 %damped.1 = f32[2592,128]{1,0:T(8,128)} custom-call(f32[2592,128]{1,0:T(8,128)S(1)} %get-tuple-element.7.a_ref, f32[36,8,128]{2,1,0:T(8,128)S(1)} %get-tuple-element.8.damp_ref), custom_call_target="tpu_custom_call" | custom-call | tf_op jit(solution)/shard_map/damped/pallas_call | solution.py:611
